TPU v7x, 128 devices: a whole 4x4x4 slice. The times are simulated.
128 devices in a mesh: ctx: 8 (over x_hi, y), tile: 16 (over z, x_lo, core).
Axes of the slice: x: 4 (x_hi: 2, x_lo: 2; x = x_hi * 2 + x_lo), y: 4, z: 4, core: 2. Of those that a mesh axis runs over, the one named last changes fastest.
Arguments:
- syndrome_bits: int32 [8, 2, 64, 512], P(None, None, 'ctx', 'tile'), may hold values from 0 to 1
- region_assign: int32 [32, 256], P('ctx', 'tile'), may hold values from 0 to 127
- state_in: bfloat16 [64, 512, 512], P('ctx', 'tile'), may hold values from -3 to 3
- bit_to_candidate: float32 [2, 512], replicated, may hold values from -5 to 5
- bit_to_gate: float32 [2, 512], replicated, may hold values from -5 to 5
- conv_weight: bfloat16 [9, 512, 512], replicated, may hold values from -0.09375 to 0.09375
- gate_weight: bfloat16 [512, 512], replicated, may hold values from -0.25 to 0.25
- gate_bias: float32 [512], replicated, may hold values from -4 to 1
- pool_weight: bfloat16 [512, 1024], replicated, may hold values from -0.25 to 0.25
- region_embed: bfloat16 [1024, 1024], P('ctx'), may hold values from -6 to 6
- attn_norm_gain: float32 [1024], replicated, may hold values from 0.1 to 1.9
- query_weight: bfloat16 [1024, 1024], replicated
- key_weight: bfloat16 [1024, 1024], replicated
- value_weight: bfloat16 [1024, 1024], replicated, may hold values from -0.1875 to 0.1875
- out_weight: bfloat16 [1024, 1024], replicated, may hold values from -0.1875 to 0.1875
- mlp_norm_gain: float32 [1024], replicated, may hold values from 0.1 to 1.9
- mlp_up: bfloat16 [1024, 2048], replicated, may hold values from -0.1875 to 0.1875
- mlp_down: bfloat16 [2048, 1024], replicated, may hold values from -0.125 to 0.125
- return_weight: bfloat16 [1024, 512], replicated, may hold values from -0.1875 to 0.1875
Outputs:
- state_out: bfloat16 [64, 512, 512], P('ctx', 'tile')
- context_out: bfloat16 [1024, 1024], P('ctx')
All inputs are finite; a program needn't handle non-finite values.
Results may differ from a plain program's by a relative error of at most 0.02.
Values may be sent and summed in bfloat16 or wider, within the bound.
A program may use at most 128 MiB of HBM per device.

v0:
```python
import math
import jax
import jax.numpy as jnp
from jax import lax
from jax.sharding import PartitionSpec as P

HEADS = 8
HDIM = 128
ROUNDS = 8


def extended(value, sides, width):
    for axis, dim in sides:
        size, length = (lax.axis_size(axis), value.shape[dim])
        up = [(i, (i + 1) % size) for i in range(size - 1)]
        down = [(j, i) for i, j in up]
        last = lax.slice_in_dim(value, length - width, length, axis=dim)
        first = lax.slice_in_dim(value, 0, width, axis=dim)
        before = lax.ppermute(last, axis, up)
        after = lax.ppermute(first, axis, down)
        value = jnp.concatenate([before, value, after], axis=dim)
    return value


def rms_norm(values, gain):
    return values * lax.rsqrt(jnp.mean(values * values, axis=-1, keepdims=True) + 1e-05) * gain


def advance(
    state, padded, syndrome_now, conv_flat, gate_weight, gate_bias, bit_to_candidate, bit_to_gate
):
    patch_rows, patch_cols, channels = state.shape
    rounded = padded[1 : patch_rows + 1, 1 : patch_cols + 1]
    columns = jnp.concatenate(
        [
            padded[offset_row : offset_row + patch_rows, offset_col : offset_col + patch_cols]
            for offset_row in range(3)
            for offset_col in range(3)
        ],
        axis=-1,
    )
    syndrome_flags = syndrome_now.astype(jnp.float32)
    drive_cand = (
        syndrome_flags[0][..., None] * bit_to_candidate[0]
        + syndrome_flags[1][..., None] * bit_to_candidate[1]
    )
    drive_gate = (
        syndrome_flags[0][..., None] * bit_to_gate[0]
        + syndrome_flags[1][..., None] * bit_to_gate[1]
    )
    candidate = (
        jnp.dot(
            columns.reshape(patch_rows * patch_cols, 9 * channels),
            conv_flat,
            preferred_element_type=jnp.float32,
        ).reshape(patch_rows, patch_cols, channels)
        + drive_cand
    )
    update_gate = jax.nn.sigmoid(
        jnp.dot(
            rounded.reshape(patch_rows * patch_cols, channels),
            gate_weight,
            preferred_element_type=jnp.float32,
        ).reshape(patch_rows, patch_cols, channels)
        + drive_gate
        + gate_bias
    )
    return state + update_gate * (jnp.tanh(candidate) - state)


def region_layer(
    tokens,
    attn_norm_gain,
    query_weight,
    key_weight,
    value_weight,
    out_weight,
    mlp_norm_gain,
    mlp_up,
    mlp_down,
    gather_keys,
):
    token_count = tokens.shape[0]
    normed = rms_norm(tokens, attn_norm_gain).astype(jnp.bfloat16)
    queries = jnp.dot(normed, query_weight, preferred_element_type=jnp.float32).astype(jnp.bfloat16)
    query_heads = queries.reshape(token_count, HEADS, HDIM).transpose(1, 0, 2)
    key_rows = jnp.dot(normed, key_weight, preferred_element_type=jnp.float32).astype(jnp.bfloat16)
    value_rows = jnp.dot(normed, value_weight, preferred_element_type=jnp.float32).astype(
        jnp.bfloat16
    )
    scale = 1.0 / math.sqrt(HDIM)

    def absorb(running, gathered, first_row):
        running_max, denominator, weighted = running
        key_part, value_part = gathered
        part_rows = key_part.shape[0]
        scores = (
            jnp.einsum(
                "hqd,khd->hqk",
                query_heads,
                key_part.reshape(part_rows, HEADS, HDIM),
                preferred_element_type=jnp.float32,
            )
            * scale
        )
        new_max = jnp.maximum(running_max, jnp.max(scores, axis=-1))
        weights = jnp.exp(scores - new_max[..., None])
        denominator = jnp.sum(weights, axis=-1)
        weighted = jnp.einsum(
            "hqk,khd->hqd",
            weights.astype(jnp.bfloat16),
            value_part.reshape(part_rows, HEADS, HDIM),
            preferred_element_type=jnp.float32,
        )
        return (new_max, denominator, weighted)

    start_state = (
        jnp.full((HEADS, token_count), -1e30, jnp.float32),
        jnp.zeros((HEADS, token_count), jnp.float32),
        jnp.zeros((HEADS, token_count, HDIM), jnp.float32),
    )
    running_max, denominator, weighted = gather_keys(key_rows, value_rows, absorb, start_state)
    attention = (
        (weighted / denominator[..., None])
        .transpose(1, 0, 2)
        .reshape(token_count, HEADS * HDIM)
        .astype(jnp.bfloat16)
    )
    attended = tokens + jnp.dot(attention, out_weight, preferred_element_type=jnp.float32)
    hidden = jax.nn.gelu(
        jnp.dot(
            rms_norm(attended, mlp_norm_gain).astype(jnp.bfloat16),
            mlp_up,
            preferred_element_type=jnp.float32,
        )
    ).astype(jnp.bfloat16)
    return (attended + jnp.dot(hidden, mlp_down, preferred_element_type=jnp.float32)).astype(
        jnp.bfloat16
    )


def local(
    syndrome_bits,
    region_assign,
    state_in,
    bit_to_candidate,
    bit_to_gate,
    conv_weight,
    gate_weight,
    gate_bias,
    pool_weight,
    region_embed,
    attn_norm_gain,
    query_weight,
    key_weight,
    value_weight,
    out_weight,
    mlp_norm_gain,
    mlp_up,
    mlp_down,
    return_weight,
):
    state = state_in.astype(jnp.float32)
    patch_rows, patch_cols, channels = state.shape
    conv_flat = conv_weight.reshape(9 * channels, channels)
    layer_weights = (
        attn_norm_gain,
        query_weight,
        key_weight,
        value_weight,
        out_weight,
        mlp_norm_gain,
        mlp_up,
        mlp_down,
    )
    context_out = None
    for round_index in range(ROUNDS):
        if round_index == ROUNDS // 2:
            pooled = (
                state.reshape(patch_rows // 2, 2, patch_cols // 2, 2, channels)
                .mean(axis=(1, 3))
                .astype(jnp.bfloat16)
            )
            band_tokens = region_embed.shape[0]
            member = (
                region_assign.reshape(1, -1) == jnp.arange(band_tokens, dtype=jnp.int32)[:, None]
            ).astype(jnp.float32)
            projected = jnp.dot(
                pooled.reshape(-1, channels), pool_weight, preferred_element_type=jnp.float32
            )
            partial_value = jnp.dot(member, projected, precision=lax.Precision.HIGHEST)
            share_rows = band_tokens // lax.axis_size("tile")
            first_row = lax.axis_index("tile") * share_rows
            summed = lax.psum_scatter(
                partial_value.astype(jnp.bfloat16), "tile", scatter_dimension=0, tiled=True
            ).astype(jnp.float32)
            embed_rows = lax.dynamic_slice_in_dim(region_embed, first_row, share_rows, 0).astype(
                jnp.float32
            )
            tokens = summed + embed_rows

            def gather_split(key_rows, value_rows, absorb, start_state):
                return absorb(
                    start_state,
                    (
                        lax.all_gather(key_rows, ("ctx", "tile"), axis=0, tiled=True),
                        lax.all_gather(value_rows, ("ctx", "tile"), axis=0, tiled=True),
                    ),
                    jnp.int32(0),
                )

            local_context = region_layer(tokens, *layer_weights, gather_split)
            context_out = lax.all_gather(local_context, "tile", axis=0, tiled=True)
            returned = jnp.dot(context_out, return_weight, preferred_element_type=jnp.float32)
            share_back = jnp.dot(member.T, returned, precision=lax.Precision.HIGHEST).reshape(
                patch_rows // 2, patch_cols // 2, channels
            )
            state = (
                state.reshape(patch_rows // 2, 2, patch_cols // 2, 2, channels)
                + share_back[:, None, :, None, :]
            ).reshape(patch_rows, patch_cols, channels)
        rounded = state.astype(jnp.bfloat16)
        padded = extended(rounded, (("ctx", 0), ("tile", 1)), 1)
        state = advance(
            state,
            padded,
            syndrome_bits[round_index],
            conv_flat,
            gate_weight,
            gate_bias,
            bit_to_candidate,
            bit_to_gate,
        )
    return (state.astype(jnp.bfloat16), context_out)


def solution(mesh):
    return jax.shard_map(
        local,
        mesh=mesh,
        in_specs=(
            P(None, None, "ctx", "tile"),
            P("ctx", "tile"),
            P("ctx", "tile", None),
            P(),
            P(),
            P(),
            P(),
            P(),
            P(),
            P("ctx", None),
            P(),
            P(),
            P(),
            P(),
            P(),
            P(),
            P(),
            P(),
            P(),
        ),
        out_specs=(P("ctx", "tile", None), P("ctx", None)),
        check_vma=False,
    )
```

profile of v0, /device:TPU:56, one launch (start us, length us, event | category | flops | bytes accessed | tf_op | source)
XLA Modules:
  0.0 692.4 jit_solution(17125236643354716497)
XLA Ops:
  8.2 2.6 collective-permute-start.1
  10.8 6.8 collective-permute-start
  20.3 1.9 collective-permute-start.2
  23.0 4.5 collective-permute-start.3
  30.0 1.4 fusion.77
  31.9 7.8 %collective-permute-start.4 = (bf16[1,32,512]{2,1,0:T(8,128)(2,1)S(1)}, bf16[1,32,512]{2,1,0:T(8,128)(2,1)S(1)}, u32[]{:S(2)}, u32[]{:S(2)}) collective-permute-start(bf16[1,32,512]{2,1,0:T(8,128)(2,1)S(1)} %get-tuple-element.46), channel_id=1, source_target_pairs={{0,16},{16,32},{32,48},{48,64},{64,80},{80,96},{96,112},{1,17},{17... | collective-permute-start | bytes 98312 | tf_op jit(solution)/shard_map/ppermute | solution.py:19
  39.7 1.9 collective-permute-start.5
  41.6 7.5 %collective-permute-done.5 = bf16[1,32,512]{2,1,0:T(8,128)(2,1)S(1)} collective-permute-done((bf16[1,32,512]{2,1,0:T(8,128)(2,1)S(1)}, bf16[1,32,512]{2,1,0:T(8,128)(2,1)S(1)}, u32[]{:S(2)}, u32[]{:S(2)}) %collective-permute-start.5) | collective-permute-done | bytes 32800 | tf_op jit(solution)/shard_map/ppermute | solution.py:20
  49.2 2.0 collective-permute-start.7
  51.2 2.3 collective-permute-start.6
  53.5 3.7 collective-permute-done.6
  57.8 1.4 fusion.75
  59.6 2.5 collective-permute-start.8
  62.2 3.3 collective-permute-start.9
  65.5 6.1 collective-permute-done.9
  71.6 1.9 collective-permute-start.11
  73.6 2.4 collective-permute-start.10
  76.0 3.6 collective-permute-done.10
  80.1 1.4 fusion.73
  82.8 1.9 collective-permute-start.12
  84.7 3.9 collective-permute-start.13
  88.7 5.5 collective-permute-done.13
  94.2 1.9 collective-permute-start.15
  96.1 2.4 collective-permute-start.14
  98.6 3.5 collective-permute-done.14
  103.3 3.8 fusion.71
  108.3 1.5 fusion.187
  111.0 53.7 %reduce-scatter.2.cloned.1.call-done = bf16[8,1024]{1,0:T(8,128)(2,1)} async-done(((bf16[128,1024]{1,0:T(8,128)(2,1)}), bf16[8,1024]{1,0:T(8,128)(2,1)}) %reduce-scatter.2.cloned.1.call-update) | async-done | bytes 16400 | tf_op jit(solution)/shard_map/reduce_scatter | solution.py:194
  166.4 2.6 convolution_convert_fusion.2
  169.2 2.6 convolution_convert_fusion.1
  171.8 196.5 %all-gather.3.cloned.1.call-done = bf16[1024,1024]{1,0:T(8,128)(2,1)} async-done(((bf16[8,1024]{1,0:T(8,128)(2,1)}), bf16[1024,1024]{1,0:T(8,128)(2,1)}) %all-gather.3.cloned.1.call-update) | async-done | bytes 2097168 | tf_op jit(solution)/shard_map/all_gather | solution.py:206
  368.4 2.6 fusion.179
  371.2 193.8 %all-gather.5.cloned.1.call-done = bf16[1024,1024]{1,0:T(8,128)(2,1)} async-done(((bf16[8,1024]{1,0:T(8,128)(2,1)}), bf16[1024,1024]{1,0:T(8,128)(2,1)}) %all-gather.5.cloned.1.call-update) | async-done | bytes 2097168 | tf_op jit(solution)/shard_map/all_gather | solution.py:207
  565.0 3.2 multiply_reduce_fusion
  568.2 4.8 fusion.88
  572.9 17.0 %all_gather.11 = bf16[128,1024]{1,0:T(8,128)(2,1)S(1)} all-gather(bf16[8,1024]{1,0:T(8,128)(2,1)S(1)} %fusion.88), channel_id=1, replica_groups=mesh['ctx'=8,'tile'=16] {'tile'}, dimensions={0}, use_global_device_ids=true | all-gather | bytes 278528 | tf_op jit(solution)/shard_map/all_gather | solution.py:213
  591.2 5.2 collective-permute-start.16
  596.4 1.9 collective-permute-start.17
  598.3 7.5 %collective-permute-done.17 = bf16[1,32,512]{2,1,0:T(8,128)(2,1)S(1)} collective-permute-done((bf16[1,32,512]{2,1,0:T(8,128)(2,1)S(1)}, bf16[1,32,512]{2,1,0:T(8,128)(2,1)S(1)}, u32[]{:S(2)}, u32[]{:S(2)}) %collective-permute-start.17) | collective-permute-done | bytes 32800 | tf_op jit(solution)/shard_map/ppermute | solution.py:20
  605.9 1.9 collective-permute-start.19
  607.8 2.4 collective-permute-start.18
  610.2 3.6 collective-permute-done.18
  614.4 3.9 fusion.69
  618.7 2.5 collective-permute-start.20
  621.2 3.4 collective-permute-start.21
  624.6 6.1 collective-permute-done.21
  630.7 1.9 collective-permute-start.23
  632.6 2.4 collective-permute-start.22
  635.0 3.6 collective-permute-done.22
  639.2 1.4 fusion.67
  641.0 1.9 collective-permute-start.24
  643.0 3.9 collective-permute-start.25
  646.9 5.5 collective-permute-done.25
  652.4 1.9 collective-permute-start.27
  654.4 2.4 collective-permute-start.26
  656.8 3.6 collective-permute-done.26
  660.9 1.4 fusion.65
  662.8 1.9 collective-permute-start.28
  664.7 3.9 collective-permute-start.29
  668.6 5.5 collective-permute-done.29
  674.2 1.9 collective-permute-start.31
  676.1 2.4 collective-permute-start.30
  678.5 3.6 collective-permute-done.30
  682.7 1.4 fusion.63
  (191 shorter events, 22.1 us)
Async XLA Ops:
  7.2 361.2 %copy-start = (bf16[1024,1024]{1,0:T(8,128)(2,1)S(1)}, bf16[1024,1024]{1,0:T(8,128)(2,1)}, u32[]{:S(2)}) copy-start(bf16[1024,1024]{1,0:T(8,128)(2,1)} %param.30) | copy-start | bytes 6291460
  7.2 22.0 %copy-start.2 = (bf16[8,32,512]{2,1,0:T(8,128)(2,1)S(1)}, bf16[8,32,512]{2,1,0:T(8,128)(2,1)}, u32[]{:S(2)}) copy-start(bf16[8,32,512]{2,1,0:T(8,128)(2,1)} %param.21) | copy-start | bytes 786436
  7.2 157.5 %reduce-scatter.2.cloned.1.call-start = ((), (), s32[]{:S(2)}) async-start(), calls=%async_computation.1 | async-start | bytes 278528 | tf_op jit(solution)/shard_map/reduce_scatter | solution.py:194
  8.2 12.0 %collective-permute-start.1 = (bf16[1,32,512]{2,1,0:T(8,128)(2,1)S(1)}, bf16[1,32,512]{2,1,0:T(8,128)(2,1)S(1)}, u32[]{:S(2)}, u32[]{:S(2)}) collective-permute-start(bf16[1,32,512]{2,1,0:T(8,128)(2,1)S(1)} %get-tuple-element.48), channel_id=1, source_target_pairs={{16,0},{32,16},{48,32},{64,48},{80,64},{96,80},{112,96},{17,1},{33... | collective-permute-start | bytes 98312 | tf_op jit(solution)/shard_map/ppermute | solution.py:20
  10.8 8.4 %collective-permute-start = (bf16[1,32,512]{2,1,0:T(8,128)(2,1)S(1)}, bf16[1,32,512]{2,1,0:T(8,128)(2,1)S(1)}, u32[]{:S(2)}, u32[]{:S(2)}) collective-permute-start(bf16[1,32,512]{2,1,0:T(8,128)(2,1)S(1)} %get-tuple-element.49), channel_id=1, source_target_pairs={{0,16},{16,32},{32,48},{48,64},{64,80},{80,96},{96,112},{1,17},{17... | collective-permute-start | bytes 98312 | tf_op jit(solution)/shard_map/ppermute | solution.py:19
  20.3 7.2 %collective-permute-start.2 = (bf16[10,1,512]{2,1,0:T(2,128)(2,1)S(1)}, bf16[10,1,512]{2,1,0:T(2,128)(2,1)S(1)}, u32[]{:S(2)}, u32[]{:S(2)}) collective-permute-start(bf16[10,1,512]{2,1,0:T(2,128)(2,1)S(1)} %get-tuple-element.33), channel_id=1, source_target_pairs={{0,1},{1,2},{2,3},{3,4},{4,5},{5,6},{6,7},{7,8},{8,9},{9,10},{10,1... | collective-permute-start | bytes 30728 | tf_op jit(solution)/shard_map/ppermute | solution.py:19
  23.0 6.0 collective-permute-start.3
  27.5 2.4 copy-start.8
  30.0 1.4 copy-start.9
  30.0 1.4 copy-start.12
  31.9 9.7 %collective-permute-start.4 = (bf16[1,32,512]{2,1,0:T(8,128)(2,1)S(1)}, bf16[1,32,512]{2,1,0:T(8,128)(2,1)S(1)}, u32[]{:S(2)}, u32[]{:S(2)}) collective-permute-start(bf16[1,32,512]{2,1,0:T(8,128)(2,1)S(1)} %get-tuple-element.46), channel_id=1, source_target_pairs={{0,16},{16,32},{32,48},{48,64},{64,80},{80,96},{96,112},{1,17},{17... | collective-permute-start | bytes 98312 | tf_op jit(solution)/shard_map/ppermute | solution.py:19
  39.7 9.4 %collective-permute-start.5 = (bf16[1,32,512]{2,1,0:T(8,128)(2,1)S(1)}, bf16[1,32,512]{2,1,0:T(8,128)(2,1)S(1)}, u32[]{:S(2)}, u32[]{:S(2)}) collective-permute-start(bf16[1,32,512]{2,1,0:T(8,128)(2,1)S(1)} %get-tuple-element.47), channel_id=1, source_target_pairs={{16,0},{32,16},{48,32},{64,48},{80,64},{96,80},{112,96},{17,1},{33... | collective-permute-start | bytes 98312 | tf_op jit(solution)/shard_map/ppermute | solution.py:20
  49.2 4.4 collective-permute-start.7
  51.2 6.0 collective-permute-start.6
  59.6 5.9 collective-permute-start.8
  62.2 9.4 %collective-permute-start.9 = (bf16[1,32,512]{2,1,0:T(8,128)(2,1)S(1)}, bf16[1,32,512]{2,1,0:T(8,128)(2,1)S(1)}, u32[]{:S(2)}, u32[]{:S(2)}) collective-permute-start(bf16[1,32,512]{2,1,0:T(8,128)(2,1)S(1)} %get-tuple-element.45), channel_id=1, source_target_pairs={{16,0},{32,16},{48,32},{64,48},{80,64},{96,80},{112,96},{17,1},{33... | collective-permute-start | bytes 98312 | tf_op jit(solution)/shard_map/ppermute | solution.py:20
  71.6 4.4 collective-permute-start.11
  73.6 6.0 collective-permute-start.10
  81.5 17.0 %copy-start.7 = (s32[4,16]{1,0:T(4,128)S(1)}, s32[4,16]{1,0:T(4,128)}, u32[]{:S(2)}) copy-start(s32[4,16]{1,0:T(4,128)} %param.20) | copy-start | bytes 772
  82.8 5.8 collective-permute-start.12
  84.7 9.4 %collective-permute-start.13 = (bf16[1,32,512]{2,1,0:T(8,128)(2,1)S(1)}, bf16[1,32,512]{2,1,0:T(8,128)(2,1)S(1)}, u32[]{:S(2)}, u32[]{:S(2)}) collective-permute-start(bf16[1,32,512]{2,1,0:T(8,128)(2,1)S(1)} %get-tuple-element.43), channel_id=1, source_target_pairs={{16,0},{32,16},{48,32},{64,48},{80,64},{96,80},{112,96},{17,1},{33... | collective-permute-start | bytes 98312 | tf_op jit(solution)/shard_map/ppermute | solution.py:20
  94.2 4.4 collective-permute-start.15
  96.1 6.0 collective-permute-start.14
  102.3 1.0 copy-start.13
  103.3 3.8 copy-start.10
  107.5 58.0 %copy-start.6 = (f32[1024]{0:T(1024)S(1)}, f32[1024]{0:T(1024)}, u32[]{:S(2)}) copy-start(f32[1024]{0:T(1024)} %param.29) | copy-start | bytes 12292
  110.9 257.5 %all-gather.3.cloned.1.call-start = ((), (), s32[]{:S(2)}) async-start(), calls=%async_computation.2 | async-start | bytes 2113536 | tf_op jit(solution)/shard_map/all_gather | solution.py:206
  169.0 396.0 %all-gather.5.cloned.1.call-start = ((), (), s32[]{:S(2)}) async-start(), calls=%async_computation.3 | async-start | bytes 2113536 | tf_op jit(solution)/shard_map/all_gather | solution.py:207
  171.8 393.2 %copy-start.4 = (bf16[8,1024]{1,0:T(8,128)(2,1)S(1)}, bf16[8,1024]{1,0:T(8,128)(2,1)}, u32[]{:S(2)}) copy-start(bf16[8,1024]{1,0:T(8,128)(2,1)} %reduce-scatter.2.cloned.1.call-done) | copy-start | bytes 49156
  371.0 197.2 %copy-start.5 = (f32[1024]{0:T(1024)S(1)}, f32[1024]{0:T(1024)}, u32[]{:S(2)}) copy-start(f32[1024]{0:T(1024)} %param.34) | copy-start | bytes 12292
  568.2 21.8 %copy-start.3 = (bf16[1024,512]{1,0:T(8,128)(2,1)S(1)}, bf16[1024,512]{1,0:T(8,128)(2,1)}, u32[]{:S(2)}) copy-start(bf16[1024,512]{1,0:T(8,128)(2,1)} %param.37) | copy-start | bytes 3145732
  591.2 7.1 %collective-permute-start.16 = (bf16[1,32,512]{2,1,0:T(8,128)(2,1)S(1)}, bf16[1,32,512]{2,1,0:T(8,128)(2,1)S(1)}, u32[]{:S(2)}, u32[]{:S(2)}) collective-permute-start(bf16[1,32,512]{2,1,0:T(8,128)(2,1)S(1)} %get-tuple-element.40), channel_id=1, source_target_pairs={{0,16},{16,32},{32,48},{48,64},{64,80},{80,96},{96,112},{1,17},{17... | collective-permute-start | bytes 98312 | tf_op jit(solution)/shard_map/ppermute | solution.py:19
  596.4 9.4 %collective-permute-start.17 = (bf16[1,32,512]{2,1,0:T(8,128)(2,1)S(1)}, bf16[1,32,512]{2,1,0:T(8,128)(2,1)S(1)}, u32[]{:S(2)}, u32[]{:S(2)}) collective-permute-start(bf16[1,32,512]{2,1,0:T(8,128)(2,1)S(1)} %get-tuple-element.41), channel_id=1, source_target_pairs={{16,0},{32,16},{48,32},{64,48},{80,64},{96,80},{112,96},{17,1},{33... | collective-permute-start | bytes 98312 | tf_op jit(solution)/shard_map/ppermute | solution.py:20
  605.9 4.4 collective-permute-start.19
  607.8 6.0 collective-permute-start.18
  614.3 3.9 copy-start.11
  614.3 24.8 %slice-start = ((s8[4718592]{0:T(1024)(128)(4,1)}), s8[4194304]{0:T(1024)(128)(4,1)S(1)}, s32[]{:S(2)}) async-start(s8[4718592]{0:T(1024)(128)(4,1)} %bitcast.207), calls=%async_computation.4 | async-start | bytes 8388608
  618.3 20.9 %slice-start.1 = ((s8[4718592]{0:T(1024)(128)(4,1)}), s8[524288]{0:T(1024)(128)(4,1)S(1)}, s32[]{:S(2)}) async-start(s8[4718592]{0:T(1024)(128)(4,1)} %bitcast.207), calls=%async_computation.5 | async-start | bytes 1048576
  618.7 5.9 collective-permute-start.20
  621.2 9.4 %collective-permute-start.21 = (bf16[1,32,512]{2,1,0:T(8,128)(2,1)S(1)}, bf16[1,32,512]{2,1,0:T(8,128)(2,1)S(1)}, u32[]{:S(2)}, u32[]{:S(2)}) collective-permute-start(bf16[1,32,512]{2,1,0:T(8,128)(2,1)S(1)} %get-tuple-element.39), channel_id=1, source_target_pairs={{16,0},{32,16},{48,32},{64,48},{80,64},{96,80},{112,96},{17,1},{33... | collective-permute-start | bytes 98312 | tf_op jit(solution)/shard_map/ppermute | solution.py:20
  630.7 4.4 collective-permute-start.23
  632.6 6.0 collective-permute-start.22
  641.0 5.9 collective-permute-start.24
  643.0 9.4 %collective-permute-start.25 = (bf16[1,32,512]{2,1,0:T(8,128)(2,1)S(1)}, bf16[1,32,512]{2,1,0:T(8,128)(2,1)S(1)}, u32[]{:S(2)}, u32[]{:S(2)}) collective-permute-start(bf16[1,32,512]{2,1,0:T(8,128)(2,1)S(1)} %get-tuple-element.37), channel_id=1, source_target_pairs={{16,0},{32,16},{48,32},{64,48},{80,64},{96,80},{112,96},{17,1},{33... | collective-permute-start | bytes 98312 | tf_op jit(solution)/shard_map/ppermute | solution.py:20
  652.4 4.4 collective-permute-start.27
  654.4 6.0 collective-permute-start.26
  662.8 5.9 collective-permute-start.28
  664.7 9.4 %collective-permute-start.29 = (bf16[1,32,512]{2,1,0:T(8,128)(2,1)S(1)}, bf16[1,32,512]{2,1,0:T(8,128)(2,1)S(1)}, u32[]{:S(2)}, u32[]{:S(2)}) collective-permute-start(bf16[1,32,512]{2,1,0:T(8,128)(2,1)S(1)} %get-tuple-element.35), channel_id=1, source_target_pairs={{16,0},{32,16},{48,32},{64,48},{80,64},{96,80},{112,96},{17,1},{33... | collective-permute-start | bytes 98312 | tf_op jit(solution)/shard_map/ppermute | solution.py:20
  674.2 4.4 collective-permute-start.31
  676.1 6.0 collective-permute-start.30
  682.7 3.3 copy-start.1
Sparse Core Ops, SparseCore 0:
  111.0 53.6 reduce-scatter.1
  169.1 199.2 all-gather.2
  370.7 194.2 all-gather.4
where the time goes:
time: 694 us; the launch traced here: 692 us
  waiting for transfers between devices  513 us (74%)
  starting transfers between devices  92.5 us (13%)
  matrix products  39.9 us (6%)
  blocking collectives  17 us (2%)
  between operations  15.2 us (2%)
  local copies, waits for them, and re-layouts  8.39 us (1%)
    all_gather x1, waiting for transfers between devices, gather_split(): lax.all_gather(key_rows, ('ctx', 'tile'), axis=0, tiled=True)  197 us
    all_gather x1, waiting for transfers between devices, gather_split(): lax.all_gather(value_rows, ('ctx', 'tile'), axis=0, tiled=True)  194 us
    reduce_scatter x1, waiting for transfers between devices, local(): lax.psum_scatter(partial_value.astype(jnp.bfloat16), 'tile', scatter_dime...  53.7 us
    ppermute x16, starting transfers between devices, extended(): before = lax.ppermute(last, axis, up)  49.2 us
    ppermute x16, waiting for transfers between devices, extended(): after = lax.ppermute(first, axis, down)  43.8 us
    ppermute x16, starting transfers between devices, extended(): after = lax.ppermute(first, axis, down)  43 us
    ppermute x16, waiting for transfers between devices, extended(): before = lax.ppermute(last, axis, up)  25 us
    all_gather x1, blocking collectives, local(): context_out = lax.all_gather(local_context, 'tile', axis=0, tiled=True)  17 us
  transfers between devices with their start and end apart: 35, of which 18 were waited for; matrix products, arithmetic and copies ran while one was open for 1% of the time, Pallas kernels for 0%

commit v1 on v0

--- a/solution.py
+++ b/solution.py
@@ -7,6 +7,13 @@
 HEADS = 8
 HDIM = 128
 ROUNDS = 8
+
+
+def gather_over(x, mesh_axis, dim):
+    devices = lax.axis_size(mesh_axis)
+    pieces = jnp.stack([x for _ in range(devices)])
+    pieces = lax.all_to_all(pieces, mesh_axis, split_axis=0, concat_axis=0)
+    return jnp.concatenate(pieces, axis=dim)
 
 
 def extended(value, sides, width):
@@ -203,7 +210,7 @@
                 return absorb(
                     start_state,
                     (
-                        lax.all_gather(key_rows, ("ctx", "tile"), axis=0, tiled=True),
+                        gather_over(key_rows, ("ctx", "tile"), 0),
                         lax.all_gather(value_rows, ("ctx", "tile"), axis=0, tiled=True),
                     ),
                     jnp.int32(0),

time: 694 us -> 512 us (0.74)
  waiting for transfers between devices: 513 us -> 262 us
  blocking collectives: 17 us -> 61.4 us
  starting transfers between devices: 92.5 us -> 113 us
    all_gather x1 -> x0, waiting for transfers between devices: 197 us -> none  [gather_split(): lax.all_gather(key_rows, ('ctx', 'tile'), axis=0, tiled=True)]
    all_to_all x0 -> x1, blocking collectives: none -> 41.8 us  [gather_over(): pieces = lax.all_to_all(pieces, mesh_axis, split_axis=0, concat_axis=0)]
    ppermute x16, waiting for transfers between devices: 43.8 us -> 5.19 us  [extended(): after = lax.ppermute(first, axis, down)]
    all_gather x1, waiting for transfers between devices: 194 us -> 163 us  [gather_split(): lax.all_gather(value_rows, ('ctx', 'tile'), axis=0, tiled=True)]
    ppermute x16, starting transfers between devices: 49.2 us -> 77.3 us  [extended(): before = lax.ppermute(last, axis, up)]
    ppermute x16, waiting for transfers between devices: 25 us -> 36.8 us  [extended(): before = lax.ppermute(last, axis, up)]
    ppermute x16, starting transfers between devices: 43 us -> 35.2 us  [extended(): after = lax.ppermute(first, axis, down)]
  transfers between devices with their start and end apart: 35 -> 34, of which waited for: 18 -> 18; matrix products, arithmetic and copies ran while one was open for 1% -> 2% of each run, Pallas kernels for 0% -> 0%
where the time goes in v1:
time: 512 us; the launch traced here: 508 us
  waiting for transfers between devices  262 us (51%)
  starting transfers between devices  113 us (22%)
  blocking collectives  61.4 us (12%)
  matrix products  39.4 us (8%)
  between operations  15.5 us (3%)
  local copies, waits for them, and re-layouts  10.6 us (2%)
  other arithmetic  6.4 us (1%)
    all_gather x1, waiting for transfers between devices, gather_split(): lax.all_gather(value_rows, ('ctx', 'tile'), axis=0, tiled=True)  163 us
    ppermute x16, starting transfers between devices, extended(): before = lax.ppermute(last, axis, up)  77.3 us
    reduce_scatter x1, waiting for transfers between devices, local(): lax.psum_scatter(partial_value.astype(jnp.bfloat16), 'tile', scatter_dime...  56.8 us
    all_to_all x1, blocking collectives, gather_over(): pieces = lax.all_to_all(pieces, mesh_axis, split_axis=0, concat_axis=0)  41.8 us
    ppermute x16, waiting for transfers between devices, extended(): before = lax.ppermute(last, axis, up)  36.8 us
    ppermute x16, starting transfers between devices, extended(): after = lax.ppermute(first, axis, down)  35.2 us
    all_gather x1, blocking collectives, local(): context_out = lax.all_gather(local_context, 'tile', axis=0, tiled=True)  19.6 us
    dot_general x8, matrix products, advance(): jnp.dot(columns.reshape(patch_rows * patch_cols, 9 * channels), conv_flat...  16.1 us
  transfers between devices with their start and end apart: 34, of which 18 were waited for; matrix products, arithmetic and copies ran while one was open for 2% of the time, Pallas kernels for 0%

profile of v1, /device:TPU:56, one launch (start us, length us, event | category | flops | bytes accessed | tf_op | source)
XLA Modules:
  0.0 507.7 jit_solution(934742488496076673)
XLA Ops:
  8.2 4.6 collective-permute-start
  12.8 1.9 collective-permute-start.1
  17.3 4.9 collective-permute-done.1
  22.2 1.9 collective-permute-start.2
  24.9 4.5 collective-permute-start.3
  33.8 1.9 collective-permute-start.5
  35.8 7.5 %collective-permute-start.4 = (bf16[1,32,512]{2,1,0:T(8,128)(2,1)S(1)}, bf16[1,32,512]{2,1,0:T(8,128)(2,1)S(1)}, u32[]{:S(2)}, u32[]{:S(2)}) collective-permute-start(bf16[1,32,512]{2,1,0:T(8,128)(2,1)S(1)} %get-tuple-element.46), channel_id=1, source_target_pairs={{0,16},{16,32},{32,48},{48,64},{64,80},{80,96},{96,112},{1,17},{17... | collective-permute-start | bytes 98312 | tf_op jit(solution)/shard_map/ppermute | solution.py:26
  43.3 1.6 collective-permute-done.4
  44.9 2.9 collective-permute-start.7
  47.9 1.9 collective-permute-start.6
  49.8 4.1 collective-permute-done.6
  54.4 1.4 fusion.74
  56.3 1.9 collective-permute-start.9
  58.2 8.1 %collective-permute-start.8 = (bf16[1,32,512]{2,1,0:T(8,128)(2,1)S(1)}, bf16[1,32,512]{2,1,0:T(8,128)(2,1)S(1)}, u32[]{:S(2)}, u32[]{:S(2)}) collective-permute-start(bf16[1,32,512]{2,1,0:T(8,128)(2,1)S(1)} %get-tuple-element.44), channel_id=1, source_target_pairs={{0,16},{16,32},{32,48},{48,64},{64,80},{80,96},{96,112},{1,17},{17... | collective-permute-start | bytes 98312 | tf_op jit(solution)/shard_map/ppermute | solution.py:26
  66.4 1.6 collective-permute-done.8
  68.0 1.9 collective-permute-start.11
  69.9 2.4 collective-permute-start.10
  72.4 3.6 collective-permute-done.10
  76.5 1.4 fusion.72
  79.2 1.9 collective-permute-start.13
  81.1 7.8 %collective-permute-start.12 = (bf16[1,32,512]{2,1,0:T(8,128)(2,1)S(1)}, bf16[1,32,512]{2,1,0:T(8,128)(2,1)S(1)}, u32[]{:S(2)}, u32[]{:S(2)}) collective-permute-start(bf16[1,32,512]{2,1,0:T(8,128)(2,1)S(1)} %get-tuple-element.42), channel_id=1, source_target_pairs={{0,16},{16,32},{32,48},{48,64},{64,80},{80,96},{96,112},{1,17},{17... | collective-permute-start | bytes 98312 | tf_op jit(solution)/shard_map/ppermute | solution.py:26
  88.9 1.6 collective-permute-done.12
  90.5 1.9 collective-permute-start.15
  92.5 2.4 collective-permute-start.14
  95.0 3.5 collective-permute-done.14
  99.7 3.8 fusion.70
  104.6 1.5 fusion.186
  107.3 56.8 %reduce-scatter.2.cloned.1.call-done = bf16[8,1024]{1,0:T(8,128)(2,1)} async-done(((bf16[128,1024]{1,0:T(8,128)(2,1)}), bf16[8,1024]{1,0:T(8,128)(2,1)}) %reduce-scatter.2.cloned.1.call-update) | async-done | bytes 16400 | tf_op jit(solution)/shard_map/reduce_scatter | solution.py:201
  165.8 2.6 convolution_convert_fusion.1
  168.5 2.0 convolution_convert_fusion.2
  170.7 41.8 %all_to_all.5 = bf16[128,8,1024]{2,1,0:T(8,128)(2,1)S(1)} all-to-all(bf16[128,8,1024]{2,1,0:T(8,128)(2,1)S(1)} %stack.2), channel_id=1, replica_groups=mesh['ctx'=8,'tile'=16] {'ctx','tile'}, dimensions={0} | all-to-all | bytes 4194304 | tf_op jit(solution)/shard_map/all_to_all | solution.py:15
  212.5 2.0 copy.25
  214.5 2.6 fusion.178
  217.3 163.0 %all-gather.2.cloned.1.call-done = bf16[1024,1024]{1,0:T(8,128)(2,1)} async-done(((bf16[8,1024]{1,0:T(8,128)(2,1)}), bf16[1024,1024]{1,0:T(8,128)(2,1)}) %all-gather.2.cloned.1.call-update) | async-done | bytes 2097168 | tf_op jit(solution)/shard_map/all_gather | solution.py:214
  380.3 3.2 multiply_reduce_fusion
  383.4 4.8 fusion.87
  388.2 19.6 %all_gather.7 = bf16[128,1024]{1,0:T(8,128)(2,1)S(1)} all-gather(bf16[8,1024]{1,0:T(8,128)(2,1)S(1)} %fusion.87), channel_id=1, replica_groups=mesh['ctx'=8,'tile'=16] {'tile'}, dimensions={0}, use_global_device_ids=true | all-gather | bytes 278528 | tf_op jit(solution)/shard_map/all_gather | solution.py:220
  409.1 1.9 collective-permute-start.17
  411.0 7.5 %collective-permute-start.16 = (bf16[1,32,512]{2,1,0:T(8,128)(2,1)S(1)}, bf16[1,32,512]{2,1,0:T(8,128)(2,1)S(1)}, u32[]{:S(2)}, u32[]{:S(2)}) collective-permute-start(bf16[1,32,512]{2,1,0:T(8,128)(2,1)S(1)} %get-tuple-element.40), channel_id=1, source_target_pairs={{0,16},{16,32},{32,48},{48,64},{64,80},{80,96},{96,112},{1,17},{17... | collective-permute-start | bytes 98312 | tf_op jit(solution)/shard_map/ppermute | solution.py:26
  418.5 1.6 collective-permute-done.16
  420.2 2.8 collective-permute-start.19
  423.0 1.9 collective-permute-start.18
  424.9 4.1 collective-permute-done.18
  429.5 3.9 fusion.68
  433.9 1.9 collective-permute-start.21
  435.8 8.1 %collective-permute-start.20 = (bf16[1,32,512]{2,1,0:T(8,128)(2,1)S(1)}, bf16[1,32,512]{2,1,0:T(8,128)(2,1)S(1)}, u32[]{:S(2)}, u32[]{:S(2)}) collective-permute-start(bf16[1,32,512]{2,1,0:T(8,128)(2,1)S(1)} %get-tuple-element.38), channel_id=1, source_target_pairs={{0,16},{16,32},{32,48},{48,64},{64,80},{80,96},{96,112},{1,17},{17... | collective-permute-start | bytes 98312 | tf_op jit(solution)/shard_map/ppermute | solution.py:26
  444.0 1.6 collective-permute-done.20
  445.6 1.9 collective-permute-start.23
  447.5 2.4 collective-permute-start.22
  450.0 3.6 collective-permute-done.22
  454.1 1.4 fusion.66
  456.0 1.9 collective-permute-start.25
  457.9 7.8 %collective-permute-start.24 = (bf16[1,32,512]{2,1,0:T(8,128)(2,1)S(1)}, bf16[1,32,512]{2,1,0:T(8,128)(2,1)S(1)}, u32[]{:S(2)}, u32[]{:S(2)}) collective-permute-start(bf16[1,32,512]{2,1,0:T(8,128)(2,1)S(1)} %get-tuple-element.36), channel_id=1, source_target_pairs={{0,16},{16,32},{32,48},{48,64},{64,80},{80,96},{96,112},{1,17},{17... | collective-permute-start | bytes 98312 | tf_op jit(solution)/shard_map/ppermute | solution.py:26
  465.8 1.6 collective-permute-done.24
  467.4 1.9 collective-permute-start.27
  469.3 2.4 collective-permute-start.26
  471.7 3.6 collective-permute-done.26
  477.7 1.9 collective-permute-start.29
  479.6 7.8 %collective-permute-start.28 = (bf16[1,32,512]{2,1,0:T(8,128)(2,1)S(1)}, bf16[1,32,512]{2,1,0:T(8,128)(2,1)S(1)}, u32[]{:S(2)}, u32[]{:S(2)}) collective-permute-start(bf16[1,32,512]{2,1,0:T(8,128)(2,1)S(1)} %get-tuple-element.34), channel_id=1, source_target_pairs={{0,16},{16,32},{32,48},{48,64},{64,80},{80,96},{96,112},{1,17},{17... | collective-permute-start | bytes 98312 | tf_op jit(solution)/shard_map/ppermute | solution.py:26
  487.5 1.6 collective-permute-done.28
  489.1 1.9 collective-permute-start.31
  491.0 2.4 collective-permute-start.30
  493.5 3.6 collective-permute-done.30
  497.6 1.4 fusion.62
  (191 shorter events, 24.9 us)
Async XLA Ops:
  7.2 207.3 %copy-start = (bf16[1024,1024]{1,0:T(8,128)(2,1)S(1)}, bf16[1024,1024]{1,0:T(8,128)(2,1)}, u32[]{:S(2)}) copy-start(bf16[1024,1024]{1,0:T(8,128)(2,1)} %param.30) | copy-start | bytes 6291460
  7.2 23.9 %copy-start.2 = (bf16[8,32,512]{2,1,0:T(8,128)(2,1)S(1)}, bf16[8,32,512]{2,1,0:T(8,128)(2,1)}, u32[]{:S(2)}) copy-start(bf16[8,32,512]{2,1,0:T(8,128)(2,1)} %param.21) | copy-start | bytes 786436
  7.2 157.0 %reduce-scatter.2.cloned.1.call-start = ((), (), s32[]{:S(2)}) async-start(), calls=%async_computation.2 | async-start | bytes 278528 | tf_op jit(solution)/shard_map/reduce_scatter | solution.py:201
  8.2 8.1 %collective-permute-start = (bf16[1,32,512]{2,1,0:T(8,128)(2,1)S(1)}, bf16[1,32,512]{2,1,0:T(8,128)(2,1)S(1)}, u32[]{:S(2)}, u32[]{:S(2)}) collective-permute-start(bf16[1,32,512]{2,1,0:T(8,128)(2,1)S(1)} %get-tuple-element.49), channel_id=1, source_target_pairs={{0,16},{16,32},{32,48},{48,64},{64,80},{80,96},{96,112},{1,17},{17... | collective-permute-start | bytes 98312 | tf_op jit(solution)/shard_map/ppermute | solution.py:26
  12.8 9.4 %collective-permute-start.1 = (bf16[1,32,512]{2,1,0:T(8,128)(2,1)S(1)}, bf16[1,32,512]{2,1,0:T(8,128)(2,1)S(1)}, u32[]{:S(2)}, u32[]{:S(2)}) collective-permute-start(bf16[1,32,512]{2,1,0:T(8,128)(2,1)S(1)} %get-tuple-element.48), channel_id=1, source_target_pairs={{16,0},{32,16},{48,32},{64,48},{80,64},{96,80},{112,96},{17,1},{33... | collective-permute-start | bytes 98312 | tf_op jit(solution)/shard_map/ppermute | solution.py:27
  22.2 7.2 %collective-permute-start.2 = (bf16[10,1,512]{2,1,0:T(2,128)(2,1)S(1)}, bf16[10,1,512]{2,1,0:T(2,128)(2,1)S(1)}, u32[]{:S(2)}, u32[]{:S(2)}) collective-permute-start(bf16[10,1,512]{2,1,0:T(2,128)(2,1)S(1)} %get-tuple-element.33), channel_id=1, source_target_pairs={{0,1},{1,2},{2,3},{3,4},{4,5},{5,6},{6,7},{7,8},{8,9},{9,10},{10,1... | collective-permute-start | bytes 30728 | tf_op jit(solution)/shard_map/ppermute | solution.py:26
  24.9 6.0 %collective-permute-start.3 = (bf16[10,1,512]{2,1,0:T(2,128)(2,1)S(1)}, bf16[10,1,512]{2,1,0:T(2,128)(2,1)S(1)}, u32[]{:S(2)}, u32[]{:S(2)}) collective-permute-start(bf16[10,1,512]{2,1,0:T(2,128)(2,1)S(1)} %get-tuple-element.32), channel_id=1, source_target_pairs={{1,0},{2,1},{3,2},{4,3},{5,4},{6,5},{7,6},{8,7},{9,8},{10,9},{11,1... | collective-permute-start | bytes 30728 | tf_op jit(solution)/shard_map/ppermute | solution.py:27
  29.5 2.4 copy-start.8
  31.9 1.4 copy-start.9
  31.9 1.4 copy-start.12
  33.8 9.5 %collective-permute-start.5 = (bf16[1,32,512]{2,1,0:T(8,128)(2,1)S(1)}, bf16[1,32,512]{2,1,0:T(8,128)(2,1)S(1)}, u32[]{:S(2)}, u32[]{:S(2)}) collective-permute-start(bf16[1,32,512]{2,1,0:T(8,128)(2,1)S(1)} %get-tuple-element.47), channel_id=1, source_target_pairs={{16,0},{32,16},{48,32},{64,48},{80,64},{96,80},{112,96},{17,1},{33... | collective-permute-start | bytes 98312 | tf_op jit(solution)/shard_map/ppermute | solution.py:27
  35.8 9.1 %collective-permute-start.4 = (bf16[1,32,512]{2,1,0:T(8,128)(2,1)S(1)}, bf16[1,32,512]{2,1,0:T(8,128)(2,1)S(1)}, u32[]{:S(2)}, u32[]{:S(2)}) collective-permute-start(bf16[1,32,512]{2,1,0:T(8,128)(2,1)S(1)} %get-tuple-element.46), channel_id=1, source_target_pairs={{0,16},{16,32},{32,48},{48,64},{64,80},{80,96},{96,112},{1,17},{17... | collective-permute-start | bytes 98312 | tf_op jit(solution)/shard_map/ppermute | solution.py:26
  44.9 4.9 collective-permute-start.7
  47.9 6.0 %collective-permute-start.6 = (bf16[10,1,512]{2,1,0:T(2,128)(2,1)S(1)}, bf16[10,1,512]{2,1,0:T(2,128)(2,1)S(1)}, u32[]{:S(2)}, u32[]{:S(2)}) collective-permute-start(bf16[10,1,512]{2,1,0:T(2,128)(2,1)S(1)} %get-tuple-element.31), channel_id=1, source_target_pairs={{0,1},{1,2},{2,3},{3,4},{4,5},{5,6},{6,7},{7,8},{8,9},{9,10},{10,1... | collective-permute-start | bytes 30728 | tf_op jit(solution)/shard_map/ppermute | solution.py:26
  56.3 10.1 %collective-permute-start.9 = (bf16[1,32,512]{2,1,0:T(8,128)(2,1)S(1)}, bf16[1,32,512]{2,1,0:T(8,128)(2,1)S(1)}, u32[]{:S(2)}, u32[]{:S(2)}) collective-permute-start(bf16[1,32,512]{2,1,0:T(8,128)(2,1)S(1)} %get-tuple-element.45), channel_id=1, source_target_pairs={{16,0},{32,16},{48,32},{64,48},{80,64},{96,80},{112,96},{17,1},{33... | collective-permute-start | bytes 98312 | tf_op jit(solution)/shard_map/ppermute | solution.py:27
  58.2 9.7 %collective-permute-start.8 = (bf16[1,32,512]{2,1,0:T(8,128)(2,1)S(1)}, bf16[1,32,512]{2,1,0:T(8,128)(2,1)S(1)}, u32[]{:S(2)}, u32[]{:S(2)}) collective-permute-start(bf16[1,32,512]{2,1,0:T(8,128)(2,1)S(1)} %get-tuple-element.44), channel_id=1, source_target_pairs={{0,16},{16,32},{32,48},{48,64},{64,80},{80,96},{96,112},{1,17},{17... | collective-permute-start | bytes 98312 | tf_op jit(solution)/shard_map/ppermute | solution.py:26
  68.0 4.4 collective-permute-start.11
  69.9 6.0 %collective-permute-start.10 = (bf16[10,1,512]{2,1,0:T(2,128)(2,1)S(1)}, bf16[10,1,512]{2,1,0:T(2,128)(2,1)S(1)}, u32[]{:S(2)}, u32[]{:S(2)}) collective-permute-start(bf16[10,1,512]{2,1,0:T(2,128)(2,1)S(1)} %get-tuple-element.27), channel_id=1, source_target_pairs={{0,1},{1,2},{2,3},{3,4},{4,5},{5,6},{6,7},{7,8},{8,9},{9,10},{10,1... | collective-permute-start | bytes 30728 | tf_op jit(solution)/shard_map/ppermute | solution.py:26
  77.9 17.0 %copy-start.7 = (s32[4,16]{1,0:T(4,128)S(1)}, s32[4,16]{1,0:T(4,128)}, u32[]{:S(2)}) copy-start(s32[4,16]{1,0:T(4,128)} %param.20) | copy-start | bytes 772
  79.2 9.8 %collective-permute-start.13 = (bf16[1,32,512]{2,1,0:T(8,128)(2,1)S(1)}, bf16[1,32,512]{2,1,0:T(8,128)(2,1)S(1)}, u32[]{:S(2)}, u32[]{:S(2)}) collective-permute-start(bf16[1,32,512]{2,1,0:T(8,128)(2,1)S(1)} %get-tuple-element.43), channel_id=1, source_target_pairs={{16,0},{32,16},{48,32},{64,48},{80,64},{96,80},{112,96},{17,1},{33... | collective-permute-start | bytes 98312 | tf_op jit(solution)/shard_map/ppermute | solution.py:27
  81.1 9.4 %collective-permute-start.12 = (bf16[1,32,512]{2,1,0:T(8,128)(2,1)S(1)}, bf16[1,32,512]{2,1,0:T(8,128)(2,1)S(1)}, u32[]{:S(2)}, u32[]{:S(2)}) collective-permute-start(bf16[1,32,512]{2,1,0:T(8,128)(2,1)S(1)} %get-tuple-element.42), channel_id=1, source_target_pairs={{0,16},{16,32},{32,48},{48,64},{64,80},{80,96},{96,112},{1,17},{17... | collective-permute-start | bytes 98312 | tf_op jit(solution)/shard_map/ppermute | solution.py:26
  90.5 4.4 collective-permute-start.15
  92.5 6.0 %collective-permute-start.14 = (bf16[10,1,512]{2,1,0:T(2,128)(2,1)S(1)}, bf16[10,1,512]{2,1,0:T(2,128)(2,1)S(1)}, u32[]{:S(2)}, u32[]{:S(2)}) collective-permute-start(bf16[10,1,512]{2,1,0:T(2,128)(2,1)S(1)} %get-tuple-element.23), channel_id=1, source_target_pairs={{0,1},{1,2},{2,3},{3,4},{4,5},{5,6},{6,7},{7,8},{8,9},{9,10},{10,1... | collective-permute-start | bytes 30728 | tf_op jit(solution)/shard_map/ppermute | solution.py:26
  98.6 1.0 copy-start.13
  99.7 3.8 copy-start.10
  103.9 61.1 %copy-start.6 = (f32[1024]{0:T(1024)S(1)}, f32[1024]{0:T(1024)}, u32[]{:S(2)}) copy-start(f32[1024]{0:T(1024)} %param.29) | copy-start | bytes 12292
  107.3 273.0 %all-gather.2.cloned.1.call-start = ((), (), s32[]{:S(2)}) async-start(), calls=%async_computation.3 | async-start | bytes 2113536 | tf_op jit(solution)/shard_map/all_gather | solution.py:214
  214.5 165.8 %copy-start.4 = (bf16[8,1024]{1,0:T(8,128)(2,1)S(1)}, bf16[8,1024]{1,0:T(8,128)(2,1)}, u32[]{:S(2)}) copy-start(bf16[8,1024]{1,0:T(8,128)(2,1)} %reduce-scatter.2.cloned.1.call-done) | copy-start | bytes 49156
  217.1 166.3 %copy-start.5 = (f32[1024]{0:T(1024)S(1)}, f32[1024]{0:T(1024)}, u32[]{:S(2)}) copy-start(f32[1024]{0:T(1024)} %param.34) | copy-start | bytes 12292
  383.4 24.4 %copy-start.3 = (bf16[1024,512]{1,0:T(8,128)(2,1)S(1)}, bf16[1024,512]{1,0:T(8,128)(2,1)}, u32[]{:S(2)}) copy-start(bf16[1024,512]{1,0:T(8,128)(2,1)} %param.37) | copy-start | bytes 3145732
  409.1 9.5 %collective-permute-start.17 = (bf16[1,32,512]{2,1,0:T(8,128)(2,1)S(1)}, bf16[1,32,512]{2,1,0:T(8,128)(2,1)S(1)}, u32[]{:S(2)}, u32[]{:S(2)}) collective-permute-start(bf16[1,32,512]{2,1,0:T(8,128)(2,1)S(1)} %get-tuple-element.41), channel_id=1, source_target_pairs={{16,0},{32,16},{48,32},{64,48},{80,64},{96,80},{112,96},{17,1},{33... | collective-permute-start | bytes 98312 | tf_op jit(solution)/shard_map/ppermute | solution.py:27
  411.0 9.1 %collective-permute-start.16 = (bf16[1,32,512]{2,1,0:T(8,128)(2,1)S(1)}, bf16[1,32,512]{2,1,0:T(8,128)(2,1)S(1)}, u32[]{:S(2)}, u32[]{:S(2)}) collective-permute-start(bf16[1,32,512]{2,1,0:T(8,128)(2,1)S(1)} %get-tuple-element.40), channel_id=1, source_target_pairs={{0,16},{16,32},{32,48},{48,64},{64,80},{80,96},{96,112},{1,17},{17... | collective-permute-start | bytes 98312 | tf_op jit(solution)/shard_map/ppermute | solution.py:26
  420.2 4.8 collective-permute-start.19
  423.0 6.0 %collective-permute-start.18 = (bf16[10,1,512]{2,1,0:T(2,128)(2,1)S(1)}, bf16[10,1,512]{2,1,0:T(2,128)(2,1)S(1)}, u32[]{:S(2)}, u32[]{:S(2)}) collective-permute-start(bf16[10,1,512]{2,1,0:T(2,128)(2,1)S(1)} %get-tuple-element.19), channel_id=1, source_target_pairs={{0,1},{1,2},{2,3},{3,4},{4,5},{5,6},{6,7},{7,8},{8,9},{9,10},{10,1... | collective-permute-start | bytes 30728 | tf_op jit(solution)/shard_map/ppermute | solution.py:26
  429.5 3.9 copy-start.11
  429.5 24.6 %slice-start = ((s8[4718592]{0:T(1024)(128)(4,1)}), s8[4194304]{0:T(1024)(128)(4,1)S(1)}, s32[]{:S(2)}) async-start(s8[4718592]{0:T(1024)(128)(4,1)} %bitcast.201), calls=%async_computation.4 | async-start | bytes 8388608
  433.4 20.6 %slice-start.1 = ((s8[4718592]{0:T(1024)(128)(4,1)}), s8[524288]{0:T(1024)(128)(4,1)S(1)}, s32[]{:S(2)}) async-start(s8[4718592]{0:T(1024)(128)(4,1)} %bitcast.201), calls=%async_computation.5 | async-start | bytes 1048576
  433.9 10.1 %collective-permute-start.21 = (bf16[1,32,512]{2,1,0:T(8,128)(2,1)S(1)}, bf16[1,32,512]{2,1,0:T(8,128)(2,1)S(1)}, u32[]{:S(2)}, u32[]{:S(2)}) collective-permute-start(bf16[1,32,512]{2,1,0:T(8,128)(2,1)S(1)} %get-tuple-element.39), channel_id=1, source_target_pairs={{16,0},{32,16},{48,32},{64,48},{80,64},{96,80},{112,96},{17,1},{33... | collective-permute-start | bytes 98312 | tf_op jit(solution)/shard_map/ppermute | solution.py:27
  435.8 9.7 %collective-permute-start.20 = (bf16[1,32,512]{2,1,0:T(8,128)(2,1)S(1)}, bf16[1,32,512]{2,1,0:T(8,128)(2,1)S(1)}, u32[]{:S(2)}, u32[]{:S(2)}) collective-permute-start(bf16[1,32,512]{2,1,0:T(8,128)(2,1)S(1)} %get-tuple-element.38), channel_id=1, source_target_pairs={{0,16},{16,32},{32,48},{48,64},{64,80},{80,96},{96,112},{1,17},{17... | collective-permute-start | bytes 98312 | tf_op jit(solution)/shard_map/ppermute | solution.py:26
  445.6 4.4 collective-permute-start.23
  447.5 6.0 %collective-permute-start.22 = (bf16[10,1,512]{2,1,0:T(2,128)(2,1)S(1)}, bf16[10,1,512]{2,1,0:T(2,128)(2,1)S(1)}, u32[]{:S(2)}, u32[]{:S(2)}) collective-permute-start(bf16[10,1,512]{2,1,0:T(2,128)(2,1)S(1)} %get-tuple-element.15), channel_id=1, source_target_pairs={{0,1},{1,2},{2,3},{3,4},{4,5},{5,6},{6,7},{7,8},{8,9},{9,10},{10,1... | collective-permute-start | bytes 30728 | tf_op jit(solution)/shard_map/ppermute | solution.py:26
  456.0 9.8 %collective-permute-start.25 = (bf16[1,32,512]{2,1,0:T(8,128)(2,1)S(1)}, bf16[1,32,512]{2,1,0:T(8,128)(2,1)S(1)}, u32[]{:S(2)}, u32[]{:S(2)}) collective-permute-start(bf16[1,32,512]{2,1,0:T(8,128)(2,1)S(1)} %get-tuple-element.37), channel_id=1, source_target_pairs={{16,0},{32,16},{48,32},{64,48},{80,64},{96,80},{112,96},{17,1},{33... | collective-permute-start | bytes 98312 | tf_op jit(solution)/shard_map/ppermute | solution.py:27
  457.9 9.4 %collective-permute-start.24 = (bf16[1,32,512]{2,1,0:T(8,128)(2,1)S(1)}, bf16[1,32,512]{2,1,0:T(8,128)(2,1)S(1)}, u32[]{:S(2)}, u32[]{:S(2)}) collective-permute-start(bf16[1,32,512]{2,1,0:T(8,128)(2,1)S(1)} %get-tuple-element.36), channel_id=1, source_target_pairs={{0,16},{16,32},{32,48},{48,64},{64,80},{80,96},{96,112},{1,17},{17... | collective-permute-start | bytes 98312 | tf_op jit(solution)/shard_map/ppermute | solution.py:26
  467.4 4.4 collective-permute-start.27
  469.3 6.0 %collective-permute-start.26 = (bf16[10,1,512]{2,1,0:T(2,128)(2,1)S(1)}, bf16[10,1,512]{2,1,0:T(2,128)(2,1)S(1)}, u32[]{:S(2)}, u32[]{:S(2)}) collective-permute-start(bf16[10,1,512]{2,1,0:T(2,128)(2,1)S(1)} %get-tuple-element.11), channel_id=1, source_target_pairs={{0,1},{1,2},{2,3},{3,4},{4,5},{5,6},{6,7},{7,8},{8,9},{9,10},{10,1... | collective-permute-start | bytes 30728 | tf_op jit(solution)/shard_map/ppermute | solution.py:26
  477.7 9.8 %collective-permute-start.29 = (bf16[1,32,512]{2,1,0:T(8,128)(2,1)S(1)}, bf16[1,32,512]{2,1,0:T(8,128)(2,1)S(1)}, u32[]{:S(2)}, u32[]{:S(2)}) collective-permute-start(bf16[1,32,512]{2,1,0:T(8,128)(2,1)S(1)} %get-tuple-element.35), channel_id=1, source_target_pairs={{16,0},{32,16},{48,32},{64,48},{80,64},{96,80},{112,96},{17,1},{33... | collective-permute-start | bytes 98312 | tf_op jit(solution)/shard_map/ppermute | solution.py:27
  479.6 9.4 %collective-permute-start.28 = (bf16[1,32,512]{2,1,0:T(8,128)(2,1)S(1)}, bf16[1,32,512]{2,1,0:T(8,128)(2,1)S(1)}, u32[]{:S(2)}, u32[]{:S(2)}) collective-permute-start(bf16[1,32,512]{2,1,0:T(8,128)(2,1)S(1)} %get-tuple-element.34), channel_id=1, source_target_pairs={{0,16},{16,32},{32,48},{48,64},{64,80},{80,96},{96,112},{1,17},{17... | collective-permute-start | bytes 98312 | tf_op jit(solution)/shard_map/ppermute | solution.py:26
  489.1 4.4 collective-permute-start.31
  491.0 6.0 %collective-permute-start.30 = (bf16[10,1,512]{2,1,0:T(2,128)(2,1)S(1)}, bf16[10,1,512]{2,1,0:T(2,128)(2,1)S(1)}, u32[]{:S(2)}, u32[]{:S(2)}) collective-permute-start(bf16[10,1,512]{2,1,0:T(2,128)(2,1)S(1)} %get-tuple-element.7), channel_id=1, source_target_pairs={{0,1},{1,2},{2,3},{3,4},{4,5},{5,6},{6,7},{7,8},{8,9},{9,10},{10,1... | collective-permute-start | bytes 30728 | tf_op jit(solution)/shard_map/ppermute | solution.py:26
  497.6 3.3 copy-start.1
Sparse Core Ops, SparseCore 0:
  107.4 56.7 reduce-scatter.1
  168.6 211.6 all-gather.1
